TPU v7x, 32 devices: a whole 2x2x4 slice. The times are simulated.
32 devices in a mesh: dp: 16 (over z, y, core), query: 2 (over x).
Axes of the slice: x: 2, y: 2, z: 4, core: 2. Of those that a mesh axis runs over, the one named last changes fastest.
Arguments:
- tokens: bfloat16 [2, 32, 128, 1280], P(None, ('dp', 'query')), may hold values from -6 to 6
- out_cotangent: bfloat16 [2, 32, 128, 1280], P(None, ('dp', 'query')), may hold values from -6 to 6
- qkv_weight: bfloat16 [1280, 3840], P('dp'), may hold values from -0.15625 to 0.15625
- out_weight: bfloat16 [1280, 1280], P('dp'), may hold values from -0.625 to 0.625
- up_weight: bfloat16 [1280, 5120], P('dp'), may hold values from -0.15625 to 0.15625
- down_weight: bfloat16 [5120, 1280], P('dp'), may hold values from -0.078125 to 0.078125
- attn_gain: bfloat16 [1280], P('dp'), may hold values from 0.5 to 1.5
- ffn_gain: bfloat16 [1280], P('dp'), may hold values from 0.5 to 1.5
- up_bias: bfloat16 [5120], P('dp'), may hold values from -3 to 3
- cell_weight: bfloat16 [1280, 5120], P('dp'), may hold values from -0.15625 to 0.15625
- gene_weight: bfloat16 [1280, 5120], P('dp'), may hold values from -0.15625 to 0.15625
- decoder_bias: bfloat16 [5120], P('dp'), may hold values from -3 to 3
- readout: bfloat16 [5120], P('dp'), may hold values from -0.15625 to 0.15625
- gene_embed: bfloat16 [2, 32, 384, 1280], P(None, ('dp', 'query')), may hold values from -6 to 6
- query_cell: int32 [2, 32, 384], P(None, ('dp', 'query')), may hold values from 0 to 1
- query_label: int32 [2, 32, 384], P(None, ('dp', 'query')), may hold values 0 or 1
- query_live: int32 [16, 2, 2], P('dp', None, 'query'), may hold values from 1 to 384, 480 in all within a row
Outputs:
- block_out: bfloat16 [2, 32, 128, 1280], P(None, ('dp', 'query'))
- grad_tokens: float32 [2, 32, 128, 1280], P(None, ('dp', 'query'))
- grad_qkv: float32 [1280, 3840], P('dp')
- grad_out: float32 [1280, 1280], P('dp')
- grad_up: float32 [1280, 5120], P('dp')
- grad_down: float32 [5120, 1280], P('dp')
- grad_attn_gain: float32 [1280], P('dp')
- grad_ffn_gain: float32 [1280], P('dp')
- grad_up_bias: float32 [5120], P('dp')
- grad_cell: float32 [1280, 5120], P('dp')
- grad_gene: float32 [1280, 5120], P('dp')
- grad_decoder_bias: float32 [5120], P('dp')
- grad_readout: float32 [5120], P('dp')
Inputs may be any that keep to these rules, and one draw needn't show every extreme that they name: `query_live`: the 2 devices of one dp index together hold 480 live rows in each micro-batch; a device's live rows are its first slots. `query_cell`: index of a cell within the query group of the row's device.
All inputs are finite; a program needn't handle non-finite values. No bound on the sum of `query_label` on one device may be relied on, other than what follows from the above.
Results may differ from a plain program's by a relative error of at most 0.02.
Values may be sent and summed in bfloat16 or wider, within the bound.
No kernel may reach another device: no remote copies, remote signals or barrier semaphores. Data moves between devices by JAX's collectives and lax.ppermute only.
A program may use at most 320 MiB of HBM per device.

v0:
```python
import jax
import jax.numpy as jnp
from jax import lax
from jax.sharding import PartitionSpec as P

D = 1280
HEADS = 20
HEAD = 64
highest = lax.Precision.HIGHEST
epsilon = 1e-05


def row_product(left, right):
    return lax.dot_general(
        left, right, (((0,), (0,)), ((), ())), preferred_element_type=jnp.float32
    )


def times_transpose(left, right):
    return lax.dot_general(
        left, right, (((1,), (1,)), ((), ())), preferred_element_type=jnp.float32
    )


def layer_stats(values):
    average = jnp.mean(values, axis=-1, keepdims=True)
    centred = values - average
    variance = jnp.mean(centred * centred, axis=-1, keepdims=True)
    inverse = lax.rsqrt(variance + epsilon)
    return (centred * inverse, inverse)


def norm_back(grad_scaled, gain, normal, inverse):
    grad_normal = grad_scaled * gain
    along_normal = jnp.mean(grad_normal * normal, axis=-1, keepdims=True)
    average = jnp.mean(grad_normal, axis=-1, keepdims=True)
    grad_values = inverse * (grad_normal - average - normal * along_normal)
    return (grad_values, jnp.sum(grad_scaled * normal, axis=0))


def encode(inputs, weights):
    qkv_weight, out_weight, up_weight, down_weight, attn_gain, ffn_gain, up_bias = weights
    length = inputs.shape[0]
    tokens_wide = inputs.astype(jnp.float32)
    norm_one, scale_one = layer_stats(tokens_wide)
    normed = (norm_one * attn_gain.astype(jnp.float32)).astype(jnp.bfloat16)
    projected = jnp.dot(normed, qkv_weight, preferred_element_type=jnp.float32).astype(jnp.bfloat16)
    projected = projected.reshape(length, 3, HEADS, HEAD)
    queries = projected[:, 0]
    key_heads = projected[:, 1]
    value_heads = projected[:, 2]
    scores = (
        jnp.einsum("qhd,khd->hqk", queries, key_heads, preferred_element_type=jnp.float32) * 0.125
    )
    row_max = jnp.max(scores, axis=-1, keepdims=True)
    shifted = jnp.exp(scores - row_max)
    row_total = jnp.sum(shifted, axis=-1, keepdims=True)
    attn_probs = (shifted / row_total).astype(jnp.bfloat16)
    logsum = row_max + jnp.log(row_total)
    mixed_heads = jnp.einsum(
        "hqk,khd->qhd", attn_probs, value_heads, preferred_element_type=jnp.float32
    )
    mixed_heads = mixed_heads.astype(jnp.bfloat16).reshape(length, D)
    hidden = tokens_wide + jnp.dot(mixed_heads, out_weight, preferred_element_type=jnp.float32)
    norm_two, scale_two = layer_stats(hidden)
    second = (norm_two * ffn_gain.astype(jnp.float32)).astype(jnp.bfloat16)
    up_proj = jnp.dot(second, up_weight, preferred_element_type=jnp.float32) + up_bias.astype(
        jnp.float32
    )
    active = jax.nn.gelu(up_proj, approximate=True).astype(jnp.bfloat16)
    output = hidden + jnp.dot(active, down_weight, preferred_element_type=jnp.float32)
    saved_state = (
        norm_one,
        scale_one,
        normed,
        queries,
        key_heads,
        value_heads,
        logsum,
        mixed_heads,
        norm_two,
        scale_two,
        second,
        up_proj,
        active,
    )
    return (output, saved_state)


def encode_back(grad_output, saved_state, weights):
    qkv_weight, out_weight, up_weight, down_weight, attn_gain, ffn_gain = weights
    (
        norm_one,
        scale_one,
        normed,
        queries,
        key_heads,
        value_heads,
        logsum,
        mixed_heads,
        norm_two,
        scale_two,
        second,
        up_proj,
        active,
    ) = saved_state
    length = grad_output.shape[0]
    grad_branch = grad_output.astype(jnp.bfloat16)
    grad_down = row_product(active, grad_branch)
    grad_active = times_transpose(grad_branch, down_weight)
    gelu_back = jax.vjp(lambda inner_values: jax.nn.gelu(inner_values, approximate=True), up_proj)[
        1
    ]
    grad_up_proj = gelu_back(grad_active)[0].astype(jnp.bfloat16)
    grad_up = row_product(second, grad_up_proj)
    grad_up_bias = jnp.sum(grad_up_proj.astype(jnp.float32), axis=0)
    grad_second = times_transpose(grad_up_proj, up_weight)
    grad_hidden_norm, grad_ffn_gain = norm_back(
        grad_second, ffn_gain.astype(jnp.float32), norm_two, scale_two
    )
    grad_hidden = grad_output + grad_hidden_norm
    grad_attn = grad_hidden.astype(jnp.bfloat16)
    grad_out = row_product(mixed_heads, grad_attn)
    grad_mixed = (
        times_transpose(grad_attn, out_weight).astype(jnp.bfloat16).reshape(length, HEADS, HEAD)
    )
    scores = (
        jnp.einsum("qhd,khd->hqk", queries, key_heads, preferred_element_type=jnp.float32) * 0.125
    )
    attn_probs = jnp.exp(scores - logsum)
    probs_low = attn_probs.astype(jnp.bfloat16)
    grad_values = jnp.einsum(
        "hqk,qhd->khd", probs_low, grad_mixed, preferred_element_type=jnp.float32
    )
    grad_probs = jnp.einsum(
        "qhd,khd->hqk", grad_mixed, value_heads, preferred_element_type=jnp.float32
    )
    along_probs = jnp.sum(grad_probs * attn_probs, axis=-1, keepdims=True)
    grad_scores = (attn_probs * (grad_probs - along_probs) * 0.125).astype(jnp.bfloat16)
    grad_queries = jnp.einsum(
        "hqk,khd->qhd", grad_scores, key_heads, preferred_element_type=jnp.float32
    )
    grad_keys = jnp.einsum("hqk,qhd->khd", grad_scores, queries, preferred_element_type=jnp.float32)
    grad_projected = (
        jnp.stack([grad_queries, grad_keys, grad_values], axis=1)
        .astype(jnp.bfloat16)
        .reshape(length, 3 * D)
    )
    grad_qkv = row_product(normed, grad_projected)
    grad_normed = times_transpose(grad_projected, qkv_weight)
    grad_input_norm, grad_attn_gain = norm_back(
        grad_normed, attn_gain.astype(jnp.float32), norm_one, scale_one
    )
    grad_input = grad_hidden + grad_input_norm
    return (
        (grad_qkv, grad_out, grad_up, grad_down, grad_attn_gain, grad_ffn_gain, grad_up_bias),
        grad_input,
    )


def decode(summary_all, weights, gene_rows, cell_ids, labels, live_count):
    cell_weight, gene_weight, decoder_bias, readout = weights
    group_size = summary_all.shape[0]
    slot_count = gene_rows.shape[0]
    cell_part = jnp.dot(summary_all, cell_weight, preferred_element_type=jnp.float32)
    onehot = (cell_ids[:, None] == jnp.arange(group_size, dtype=jnp.int32)[None, :]).astype(
        jnp.float32
    )
    picked = jnp.dot(onehot, cell_part, precision=highest)
    pre_act = (
        picked
        + jnp.dot(gene_rows, gene_weight, preferred_element_type=jnp.float32)
        + decoder_bias.astype(jnp.float32)
    )
    activity, silu_back = jax.vjp(jax.nn.silu, pre_act)
    read_wide = readout.astype(jnp.float32)
    logits = jnp.sum(activity * read_wide[None, :], axis=-1)
    live_rows = (jnp.arange(slot_count, dtype=jnp.int32) < live_count).astype(jnp.float32)
    grad_logits = live_rows * (jax.nn.sigmoid(logits) - labels.astype(jnp.float32))
    grad_readout = jnp.sum(grad_logits[:, None] * activity, axis=0)
    grad_pre = silu_back(grad_logits[:, None] * read_wide[None, :])[0].astype(jnp.bfloat16)
    grad_pre_wide = grad_pre.astype(jnp.float32)
    grad_decoder_bias = jnp.sum(grad_pre_wide, axis=0)
    grad_gene = row_product(gene_rows, grad_pre)
    grad_cellproj = lax.dot_general(
        onehot, grad_pre_wide, (((0,), (0,)), ((), ())), precision=highest
    )
    grad_cell = lax.dot_general(
        summary_all.astype(jnp.float32), grad_cellproj, (((0,), (0,)), ((), ())), precision=highest
    )
    grad_summary = lax.dot_general(
        grad_cellproj, cell_weight.astype(jnp.float32), (((1,), (1,)), ((), ())), precision=highest
    )
    return ((grad_cell, grad_gene, grad_decoder_bias, grad_readout), grad_summary)


def shards(
    tokens,
    out_cotangent,
    qkv_weight,
    out_weight,
    up_weight,
    down_weight,
    attn_gain,
    ffn_gain,
    up_bias,
    cell_weight,
    gene_weight,
    decoder_bias,
    readout,
    gene_embed,
    query_cell,
    query_label,
    query_live,
):
    micro_count = tokens.shape[0]
    outputs = []
    input_grads = []
    totals = None
    for micro_index in range(micro_count):
        gathered = (
            lax.all_gather(qkv_weight, "dp", axis=0, tiled=True),
            lax.all_gather(out_weight, "dp", axis=0, tiled=True),
            lax.all_gather(up_weight, "dp", axis=0, tiled=True),
            lax.all_gather(down_weight, "dp", axis=0, tiled=True),
            lax.all_gather(attn_gain, "dp", axis=0, tiled=True),
            lax.all_gather(ffn_gain, "dp", axis=0, tiled=True),
            lax.all_gather(up_bias, "dp", axis=0, tiled=True),
            lax.all_gather(cell_weight, "dp", axis=0, tiled=True),
            lax.all_gather(gene_weight, "dp", axis=0, tiled=True),
            lax.all_gather(decoder_bias, "dp", axis=0, tiled=True),
            lax.all_gather(readout, "dp", axis=0, tiled=True),
        )
        output, saved_state = encode(tokens[micro_index, 0], gathered[:7])
        outputs.append(output.astype(jnp.bfloat16))
        summary_all = lax.all_gather(output[0:1].astype(jnp.bfloat16), "query", axis=0, tiled=True)
        decoder_grads, grad_summary = decode(
            summary_all,
            gathered[7:],
            gene_embed[micro_index, 0],
            query_cell[micro_index, 0],
            query_label[micro_index, 0],
            query_live[0, micro_index, 0],
        )
        grad_own = lax.psum_scatter(
            grad_summary.astype(jnp.bfloat16), "query", scatter_dimension=0, tiled=True
        ).astype(jnp.float32)
        grad_output = out_cotangent[micro_index, 0].astype(jnp.float32)
        grad_output = grad_output.at[0:1].add(grad_own)
        back_weights = (
            lax.all_gather(qkv_weight, "dp", axis=0, tiled=True),
            lax.all_gather(out_weight, "dp", axis=0, tiled=True),
            lax.all_gather(up_weight, "dp", axis=0, tiled=True),
            lax.all_gather(down_weight, "dp", axis=0, tiled=True),
            lax.all_gather(attn_gain, "dp", axis=0, tiled=True),
            lax.all_gather(ffn_gain, "dp", axis=0, tiled=True),
        )
        encoder_grads, grad_input = encode_back(grad_output, saved_state, back_weights)
        input_grads.append(grad_input)
        step_grads = encoder_grads + decoder_grads
        if micro_index == 0:
            totals = tuple(step_grads)
        else:
            totals = tuple((earlier + later for earlier, later in zip(totals, step_grads)))
    owned = (
        lax.psum_scatter(
            totals[0].astype(jnp.bfloat16), "dp", scatter_dimension=0, tiled=True
        ).astype(jnp.float32),
        lax.psum_scatter(
            totals[1].astype(jnp.bfloat16), "dp", scatter_dimension=0, tiled=True
        ).astype(jnp.float32),
        lax.psum_scatter(
            totals[2].astype(jnp.bfloat16), "dp", scatter_dimension=0, tiled=True
        ).astype(jnp.float32),
        lax.psum_scatter(
            totals[3].astype(jnp.bfloat16), "dp", scatter_dimension=0, tiled=True
        ).astype(jnp.float32),
        lax.psum_scatter(
            totals[4].astype(jnp.bfloat16), "dp", scatter_dimension=0, tiled=True
        ).astype(jnp.float32),
        lax.psum_scatter(
            totals[5].astype(jnp.bfloat16), "dp", scatter_dimension=0, tiled=True
        ).astype(jnp.float32),
        lax.psum_scatter(
            totals[6].astype(jnp.bfloat16), "dp", scatter_dimension=0, tiled=True
        ).astype(jnp.float32),
        lax.psum_scatter(
            totals[7].astype(jnp.bfloat16), "dp", scatter_dimension=0, tiled=True
        ).astype(jnp.float32),
        lax.psum_scatter(
            totals[8].astype(jnp.bfloat16), "dp", scatter_dimension=0, tiled=True
        ).astype(jnp.float32),
        lax.psum_scatter(
            totals[9].astype(jnp.bfloat16), "dp", scatter_dimension=0, tiled=True
        ).astype(jnp.float32),
        lax.psum_scatter(
            totals[10].astype(jnp.bfloat16), "dp", scatter_dimension=0, tiled=True
        ).astype(jnp.float32),
    )
    totals = (
        lax.psum(owned[0].astype(jnp.bfloat16), "query").astype(jnp.float32),
        lax.psum(owned[1].astype(jnp.bfloat16), "query").astype(jnp.float32),
        lax.psum(owned[2].astype(jnp.bfloat16), "query").astype(jnp.float32),
        lax.psum(owned[3].astype(jnp.bfloat16), "query").astype(jnp.float32),
        lax.psum(owned[4].astype(jnp.bfloat16), "query").astype(jnp.float32),
        lax.psum(owned[5].astype(jnp.bfloat16), "query").astype(jnp.float32),
        lax.psum(owned[6].astype(jnp.bfloat16), "query").astype(jnp.float32),
        lax.psum(owned[7].astype(jnp.bfloat16), "query").astype(jnp.float32),
        lax.psum(owned[8].astype(jnp.bfloat16), "query").astype(jnp.float32),
        lax.psum(owned[9].astype(jnp.bfloat16), "query").astype(jnp.float32),
        lax.psum(owned[10].astype(jnp.bfloat16), "query").astype(jnp.float32),
    )
    block_out = jnp.stack(outputs, axis=0)[:, None]
    grad_tokens = jnp.stack(input_grads, axis=0)[:, None]
    return (
        block_out,
        grad_tokens,
        totals[0],
        totals[1],
        totals[2],
        totals[3],
        totals[4],
        totals[5],
        totals[6],
        totals[7],
        totals[8],
        totals[9],
        totals[10],
    )


def solution(mesh):
    placed = (
        P(None, ("dp", "query"), None, None),
        P(None, ("dp", "query"), None, None),
        P("dp", None),
        P("dp", None),
        P("dp", None),
        P("dp", None),
        P("dp"),
        P("dp"),
        P("dp"),
        P("dp", None),
        P("dp", None),
        P("dp"),
        P("dp"),
        P(None, ("dp", "query"), None, None),
        P(None, ("dp", "query"), None),
        P(None, ("dp", "query"), None),
        P("dp", None, "query"),
    )
    return jax.shard_map(
        shards,
        mesh=mesh,
        in_specs=placed,
        out_specs=(
            P(None, ("dp", "query"), None, None),
            P(None, ("dp", "query"), None, None),
            P("dp", None),
            P("dp", None),
            P("dp", None),
            P("dp", None),
            P("dp"),
            P("dp"),
            P("dp"),
            P("dp", None),
            P("dp", None),
            P("dp"),
            P("dp"),
        ),
        check_vma=False,
    )
```

profile of v0, /device:TPU:0, one launch (start us, length us, event | category | flops | bytes accessed | tf_op | source)
XLA Modules:
  0.0 1549.0 jit_solution(1948422574728645002)
XLA Ops:
  14.5 65.3 %all-reduce.13 = (bf16[1280]{0:T(1024)(128)(2,1)S(1)}, bf16[5120]{0:T(1024)(128)(2,1)S(1)}, bf16[1280]{0:T(1024)(128)(2,1)S(1)}, bf16[5120]{0:T(1024)(128)(2,1)S(1)}, bf16[5120]{0:T(1024)(128)(2,1)S(1)}) all-reduce(bf16[1280]{0:T(1024)(128)(2,1)S(1)} %dynamic-update-slice.6, ...), channel_id=1, replica_groups=mesh['dp'=16,'query'=2] {'dp'}, use_global_device_ids=true, to_apply=%add | all-reduce | flops 17920 | bytes 71680
  81.0 16.6 %all-gather.9.cloned.1.call-done = bf16[1280,3840]{1,0:T(8,128)(2,1)} async-done(((bf16[80,3840]{1,0:T(8,128)(2,1)}), bf16[1280,3840]{1,0:T(8,128)(2,1)}) %all-gather.9.cloned.1.call-update) | async-done | bytes 9830416 | tf_op jit(solution)/shard_map/all_gather | solution.py:222
  97.6 5.3 convolution_convert_fusion
  103.7 5.9 convolution_convert_fusion.1
  112.9 31.2 %all-gather.11.cloned.1.call-done = bf16[1280,1280]{1,0:T(8,128)(2,1)} async-done(((bf16[80,1280]{1,0:T(8,128)(2,1)}), bf16[1280,1280]{1,0:T(8,128)(2,1)}) %all-gather.11.cloned.1.call-update) | async-done | bytes 3276816 | tf_op jit(solution)/shard_map/all_gather | solution.py:223
  144.1 2.7 fusion.191
  151.0 98.3 %all-gather.13.cloned.1.call-done = bf16[1280,5120]{1,0:T(8,128)(2,1)} async-done(((bf16[80,5120]{1,0:T(8,128)(2,1)}), bf16[1280,5120]{1,0:T(8,128)(2,1)}) %all-gather.13.cloned.1.call-update) | async-done | bytes 13107216 | tf_op jit(solution)/shard_map/all_gather | solution.py:224
  249.3 8.2 convolution_add_fusion.1
  257.5 96.1 %all-gather.15.cloned.1.call-done = bf16[5120,1280]{1,0:T(8,128)(2,1)} async-done(((bf16[320,1280]{1,0:T(8,128)(2,1)}), bf16[5120,1280]{1,0:T(8,128)(2,1)}) %all-gather.15.cloned.1.call-update) | async-done | bytes 13107216 | tf_op jit(solution)/shard_map/all_gather | solution.py:225
  353.6 8.0 fusion.27
  361.6 4.7 all-gather.1
  366.3 2.0 convolution_add_fusion.2
  368.4 2.4 fusion.26
  370.8 4.4 all-gather
  375.1 82.8 %all-gather.17.cloned.1.call-done = bf16[1280,5120]{1,0:T(8,128)(2,1)} async-done(((bf16[80,5120]{1,0:T(8,128)(2,1)}), bf16[1280,5120]{1,0:T(8,128)(2,1)}) %all-gather.17.cloned.1.call-update) | async-done | bytes 13107216 | tf_op jit(solution)/shard_map/all_gather | solution.py:229
  457.9 6.5 fusion.165
  464.5 97.8 %all-gather.19.cloned.1.call-done = bf16[1280,5120]{1,0:T(8,128)(2,1)} async-done(((bf16[80,5120]{1,0:T(8,128)(2,1)}), bf16[1280,5120]{1,0:T(8,128)(2,1)}) %all-gather.19.cloned.1.call-update) | async-done | bytes 13107216 | tf_op jit(solution)/shard_map/all_gather | solution.py:230
  562.3 10.5 fusion.49
  572.8 6.2 add_add_fusion
  579.1 12.6 fusion.53
  591.8 1.8 fusion.169
  593.6 9.9 multiply_reduce_fusion.3
  604.8 11.1 convert_reduce_fusion.1
  615.9 12.7 fusion.51
  628.6 16.2 %fusion.2 = bf16[1280,5120]{0,1:T(8,128)(2,1)} fusion(f32[5120,1280]{1,0:T(8,128)} %fusion.51, bf16[384,5120]{1,0:T(8,128)(2,1)} %get-tuple-element.137, bf16[2,1,384,1280]{3,2,1,0:T(8,128)(2,1)} %param.34), kind=kOutput, calls=%fused_computation.7 | convolution fusion | flops 5046272000 | bytes 44236800 | tf_op jit(solution)/shard_map/dot_general | solution.py:14
  644.8 17.6 %copy.89 = bf16[1280,5120]{1,0:T(8,128)(2,1)} copy(bf16[1280,5120]{0,1:T(8,128)(2,1)} %fusion.2) | data formatting | bytes 26214400
  663.7 2.1 slice_convert_fusion.1
  665.8 3.1 fusion.135
  670.4 14.2 convolution_convert_fusion.5
  684.5 13.5 convolution_convert_fusion.4
  698.0 8.3 all-reduce.15
  708.9 11.2 convert_reduce_fusion.3
  720.1 10.6 multiply_reduce_fusion.7
  730.7 9.7 convert_reduce_fusion.2
  740.5 10.3 multiply_reduce_fusion.6
  753.1 2.7 fusion.11
  757.7 3.0 convolution_convert_fusion.3
  760.8 1.9 copy.70
  762.6 3.0 convolution_convert_fusion.2
  769.5 2.2 convolution_bitcast_fusion.5
  771.7 3.2 convolution_bitcast_fusion.4
  774.9 2.4 fusion.133
  777.3 3.1 convolution_bitcast_fusion.2
  780.4 3.1 convolution_bitcast_fusion.1
  786.1 8.3 fusion.116
  794.5 11.1 add_convert_fusion.4
  806.7 12.7 fusion.185
  819.5 15.7 %add_convert_fusion.3 = bf16[1280,5120]{1,0:T(8,128)(2,1)} fusion(f32[1280,5120]{1,0:T(8,128)} %fusion.185, bf16[128,5120]{1,0:T(8,128)(2,1)} %copy-done.26, f32[128,1280]{1,0:T(8,128)S(1)} %copy-done.6, f32[128]{0:T(128)S(1)} %copy-done.75, f32[128]{0:T(128)S(1)} %copy-done.70, f32[1280]{0:T(1024)S(1)} %convert_element_type.331), kind=kOutput, calls=%fused_computation.5 | convolution fusion | flops 1691484160 | bytes 41293824 | tf_op jit(solution)/shard_map/dot_general | solution.py:14
  836.3 12.8 fusion.146
  849.1 16.3 %add_convert_fusion.2 = bf16[5120,1280]{1,0:T(8,128)(2,1)} fusion(f32[5120,1280]{1,0:T(8,128)} %fusion.146, f32[128,1280]{1,0:T(8,128)S(1)} %copy-done.22, f32[128,5120]{1,0:T(8,128)} %convolution_add_fusion.1), kind=kOutput, calls=%fused_computation.4 | convolution fusion | flops 1696890880 | bytes 42598400 | tf_op jit(solution)/shard_map/dot_general | solution.py:14
  866.1 13.9 fusion.167
  880.0 19.8 %add_convert_fusion.1 = bf16[1280,5120]{1,0:T(8,128)(2,1)} fusion(f32[1280,5120]{1,0:T(8,128)} %fusion.167, f32[2,5120]{1,0:T(2,128)S(1)} %fusion.134, bf16[2,1,1280]{2,1,0:T(2,128)(2,1)S(1)} %copy-done.61), kind=kOutput, calls=%fused_computation.3 | convolution fusion | flops 170393600 | bytes 39367680 | tf_op jit(solution)/shard_map/dot_general | solution.py:188
  901.2 2.3 copy.90
  903.5 83.3 %reduce-scatter.9.cloned.1.call-done = bf16[80,3840]{1,0:T(8,128)(2,1)} async-done(((bf16[1280,3840]{1,0:T(8,128)(2,1)}), bf16[80,3840]{1,0:T(8,128)(2,1)}) %reduce-scatter.9.cloned.1.call-update) | async-done | bytes 614416 | tf_op jit(solution)/shard_map/reduce_scatter | solution.py:266
  986.8 142.1 %reduce-scatter.13.cloned.1.call-done = bf16[80,5120]{1,0:T(8,128)(2,1)} async-done(((bf16[1280,5120]{1,0:T(8,128)(2,1)}), bf16[80,5120]{1,0:T(8,128)(2,1)}) %reduce-scatter.13.cloned.1.call-update) | async-done | bytes 819216 | tf_op jit(solution)/shard_map/reduce_scatter | solution.py:272
  1128.9 142.2 %reduce-scatter.15.cloned.1.call-done = bf16[320,1280]{1,0:T(8,128)(2,1)} async-done(((bf16[5120,1280]{1,0:T(8,128)(2,1)}), bf16[320,1280]{1,0:T(8,128)(2,1)}) %reduce-scatter.15.cloned.1.call-update) | async-done | bytes 819216 | tf_op jit(solution)/shard_map/reduce_scatter | solution.py:275
  1271.1 141.5 %reduce-scatter.17.cloned.1.call-done = bf16[80,5120]{1,0:T(8,128)(2,1)} async-done(((bf16[1280,5120]{1,0:T(8,128)(2,1)}), bf16[80,5120]{1,0:T(8,128)(2,1)}) %reduce-scatter.17.cloned.1.call-update) | async-done | bytes 819216 | tf_op jit(solution)/shard_map/reduce_scatter | solution.py:287
  1412.6 7.2 fusion.194
  1419.9 8.4 fusion.81
  1428.5 59.6 %all-reduce.12 = (bf16[1280]{0:T(1024)(128)(2,1)S(1)}, bf16[1280]{0:T(1024)(128)(2,1)S(1)}, bf16[5120]{0:T(1024)(128)(2,1)S(1)}, bf16[5120]{0:T(1024)(128)(2,1)S(1)}, bf16[5120]{0:T(1024)(128)(2,1)S(1)}) all-reduce(bf16[1280]{0:T(1024)(128)(2,1)S(1)} %add_convert_fusion.9, ...), channel_id=8, replica_groups=mesh['dp'=16,'query'=2] {'dp'}, use_global_device_ids=true, to_apply=%region_36.37.clone | all-reduce | flops 17920 | bytes 71680
  1488.5 5.0 all-reduce.14
  1497.2 1.6 fusion.80
  1499.9 33.9 %all-reduce.19.cloned.1.call-done = (bf16[80,5120]{0,1:T(8,128)(2,1)}, bf16[80,3840]{1,0:T(8,128)(2,1)}, bf16[80,1280]{1,0:T(8,128)(2,1)}, bf16[80,5120]{1,0:T(8...) async-done(((bf16[80,5120]{0,1:T(8,128)(2,1)}, bf16[80,3840]{1,0:T(8,128)(2,1)}, bf16[80,1280]{1,0:T(8,128)(2,1)}, bf16[80,5120]{1,0:T(8,128)(2,1)}, ...) | async-done | bytes 4096016 | tf_op jit(solution)/shard_map/psum | solution.py:309
  1533.8 2.6 convert_element_type.387
  (319 shorter events, 46.4 us)
Async XLA Ops:
  7.2 72.5 %copy-start.85 = (s32[1,2,1]{1,2,0:T(1,128)S(1)}, s32[1,2,1]{1,2,0:T(1,128)}, u32[]{:S(2)}) copy-start(s32[1,2,1]{1,2,0:T(1,128)} %param.37) | copy-start | bytes 28
  7.3 73.1 %copy-start.82 = (s32[2,1,384]{2,1,0:T(1,128)S(1)}, s32[2,1,384]{2,1,0:T(1,128)}, u32[]{:S(2)}) copy-start(s32[2,1,384]{2,1,0:T(1,128)} %param.35) | copy-start | bytes 9220
  7.3 73.1 %copy-start.83 = (s32[2,1,384]{2,1,0:T(1,128)S(1)}, s32[2,1,384]{2,1,0:T(1,128)}, u32[]{:S(2)}) copy-start(s32[2,1,384]{2,1,0:T(1,128)} %param.36) | copy-start | bytes 9220
  7.3 73.2 %copy-start.7 = (bf16[2,1,128,1280]{3,2,1,0:T(8,128)(2,1)S(1)}, bf16[2,1,128,1280]{3,2,1,0:T(8,128)(2,1)}, u32[]{:S(2)}) copy-start(bf16[2,1,128,1280]{3,2,1,0:T(8,128)(2,1)} %param.21) | copy-start | bytes 1966084
  7.3 90.3 %all-gather.9.cloned.1.call-start = ((), (), s32[]{:S(2)}) async-start(), calls=%async_computation.6 | async-start | bytes 10444800 | tf_op jit(solution)/shard_map/all_gather | solution.py:222
  8.0 136.1 %all-gather.11.cloned.1.call-start = ((), (), s32[]{:S(2)}) async-start(), calls=%async_computation.7 | async-start | bytes 3481600 | tf_op jit(solution)/shard_map/all_gather | solution.py:223
  8.8 240.5 %all-gather.13.cloned.1.call-start = ((), (), s32[]{:S(2)}) async-start(), calls=%async_computation.8 | async-start | bytes 13926400 | tf_op jit(solution)/shard_map/all_gather | solution.py:224
  9.5 344.1 %all-gather.15.cloned.1.call-start = ((), (), s32[]{:S(2)}) async-start(), calls=%async_computation.9 | async-start | bytes 13926400 | tf_op jit(solution)/shard_map/all_gather | solution.py:225
  10.1 447.9 %all-gather.17.cloned.1.call-start = ((), (), s32[]{:S(2)}) async-start(), calls=%async_computation.10 | async-start | bytes 13926400 | tf_op jit(solution)/shard_map/all_gather | solution.py:229
  10.7 551.6 %all-gather.19.cloned.1.call-start = ((), (), s32[]{:S(2)}) async-start(), calls=%async_computation.11 | async-start | bytes 13926400 | tf_op jit(solution)/shard_map/all_gather | solution.py:230
  11.2 889.9 %reduce-scatter.19.cloned.1.call-start = ((), (), s32[]{:S(2)}) async-start(), calls=%async_computation.17 | async-start | bytes 13926400
  79.8 23.9 %copy-start.43 = (f32[1280]{0:T(1024)}, f32[1280]{0:T(1024)S(1)}, u32[]{:S(2)}) copy-start(f32[1280]{0:T(1024)S(1)} %convert_element_type.325) | copy-start | bytes 15364
  80.6 22.3 %copy-start.76 = (f32[128]{0:T(128)}, f32[128]{0:T(128)S(1)}, u32[]{:S(2)}) copy-start(f32[128]{0:T(128)S(1)} %get-tuple-element.159) | copy-start | bytes 1540
  80.6 23.0 %copy-start.71 = (f32[128]{0:T(128)}, f32[128]{0:T(128)S(1)}, u32[]{:S(2)}) copy-start(f32[128]{0:T(128)S(1)} %get-tuple-element.160) | copy-start | bytes 1540
  81.0 22.0 %copy-start.80 = (f32[128]{0:T(128)}, f32[128]{0:T(128)S(1)}, u32[]{:S(2)}) copy-start(f32[128]{0:T(128)S(1)} %add_rsqrt_fusion.1) | copy-start | bytes 1540
  81.0 22.6 %copy-start.78 = (f32[128]{0:T(128)}, f32[128]{0:T(128)S(1)}, u32[]{:S(2)}) copy-start(f32[128]{0:T(128)S(1)} %add_rsqrt_fusion.3) | copy-start | bytes 1540
  112.9 34.1 %copy-start.38 = (bf16[20,64,128]{2,1,0:T(8,128)(2,1)}, bf16[20,64,128]{2,1,0:T(8,128)(2,1)S(1)}, u32[]{:S(2)}) copy-start(bf16[20,64,128]{2,1,0:T(8,128)(2,1)S(1)} %convolution_convert_fusion.6) | copy-start | bytes 983044
  146.8 605.1 %copy-start.5 = (f32[128,1280]{1,0:T(8,128)}, f32[128,1280]{1,0:T(8,128)S(1)}, u32[]{:S(2)}) copy-start(f32[128,1280]{1,0:T(8,128)S(1)} %get-tuple-element.146) | copy-start | bytes 1966084
  146.8 102.5 %copy-start.69 = (f32[128]{0:T(128)}, f32[128]{0:T(128)S(1)}, u32[]{:S(2)}) copy-start(f32[128]{0:T(128)S(1)} %broadcast_multiply_fusion.8) | copy-start | bytes 1540
  150.7 589.7 %copy-start.9 = (f32[128,1280]{1,0:T(8,128)}, f32[128,1280]{1,0:T(8,128)S(1)}, u32[]{:S(2)}) copy-start(f32[128,1280]{1,0:T(8,128)S(1)} %get-tuple-element.150) | copy-start | bytes 1966084
  151.0 106.5 %copy-start.74 = (f32[128]{0:T(128)}, f32[128]{0:T(128)S(1)}, u32[]{:S(2)}) copy-start(f32[128]{0:T(128)S(1)} %add_rsqrt_fusion) | copy-start | bytes 1540
  353.6 12.7 copy-start
  353.6 14.7 slice-start.4
  353.6 14.7 slice-start.5
  353.6 14.7 slice-start.6
  366.3 91.6 %copy-start.60 = (bf16[2,1,1280]{2,1,0:T(2,128)(2,1)}, bf16[2,1,1280]{2,1,0:T(2,128)(2,1)S(1)}, u32[]{:S(2)}) copy-start(bf16[2,1,1280]{2,1,0:T(2,128)(2,1)S(1)} %all-gather.1) | copy-start | bytes 15364
  370.8 93.7 %copy-start.47 = (bf16[128,1280]{1,0:T(8,128)(2,1)}, bf16[128,1280]{1,0:T(8,128)(2,1)S(1)}, u32[]{:S(2)}) copy-start(bf16[128,1280]{1,0:T(8,128)(2,1)S(1)} %fusion.26) | copy-start | bytes 983044
  375.1 216.6 %copy-start.62 = (bf16[2,1,1280]{2,1,0:T(2,128)(2,1)}, bf16[2,1,1280]{2,1,0:T(2,128)(2,1)S(1)}, u32[]{:S(2)}) copy-start(bf16[2,1,1280]{2,1,0:T(2,128)(2,1)S(1)} %all-gather) | copy-start | bytes 15364
  572.8 18.9 %slice-start = ((s8[13107200]{0:T(1024)(128)(4,1)}), s8[4194304]{0:T(1024)(128)(4,1)S(1)}, s32[]{:S(2)}) async-start(s8[13107200]{0:T(1024)(128)(4,1)} %bitcast.251), calls=%async_computation.19 | async-start | bytes 8388608
  572.8 18.9 %slice-start.1 = ((s8[13107200]{0:T(1024)(128)(4,1)}), s8[4194304]{0:T(1024)(128)(4,1)S(1)}, s32[]{:S(2)}) async-start(s8[13107200]{0:T(1024)(128)(4,1)} %bitcast.251), calls=%async_computation.20 | async-start | bytes 8388608
  579.1 12.7 slice-start.2
  579.1 12.7 slice-start.3
  615.9 12.7 copy-start.4
  662.5 241.1 %reduce-scatter.11.cloned.1.call-start = ((), (), s32[]{:S(2)}) async-start(), calls=%async_computation.13 | async-start | bytes 3481600 | tf_op jit(solution)/shard_map/reduce_scatter | solution.py:269
  707.9 44.0 %copy-start.21 = (f32[128,1280]{1,0:T(8,128)}, f32[128,1280]{1,0:T(8,128)S(1)}, u32[]{:S(2)}) copy-start(f32[128,1280]{1,0:T(8,128)S(1)} %scatter-add.9) | copy-start | bytes 1966084
  708.9 31.6 %copy-start.23 = (f32[128,1280]{1,0:T(8,128)}, f32[128,1280]{1,0:T(8,128)S(1)}, u32[]{:S(2)}) copy-start(f32[128,1280]{1,0:T(8,128)S(1)} %scatter-add.6) | copy-start | bytes 1966084
  720.1 10.6 copy-start.25
  720.1 10.6 copy-start.11
  730.7 9.8 copy-start.70
  730.7 9.8 copy-start.75
  740.5 10.4 copy-start.26
  740.5 10.4 copy-start.34
  755.8 231.0 %reduce-scatter.9.cloned.1.call-start = ((), (), s32[]{:S(2)}) async-start(), calls=%async_computation.12 | async-start | bytes 10444800 | tf_op jit(solution)/shard_map/reduce_scatter | solution.py:266
  785.4 9.1 copy-start.27
  786.1 8.4 copy-start.77
  786.1 8.4 copy-start.81
  805.6 13.8 copy-start.6
  805.7 323.3 %reduce-scatter.13.cloned.1.call-start = ((), (), s32[]{:S(2)}) async-start(), calls=%async_computation.14 | async-start | bytes 13926400 | tf_op jit(solution)/shard_map/reduce_scatter | solution.py:272
  835.2 13.9 copy-start.22
  835.2 435.9 %reduce-scatter.15.cloned.1.call-start = ((), (), s32[]{:S(2)}) async-start(), calls=%async_computation.15 | async-start | bytes 13926400 | tf_op jit(solution)/shard_map/reduce_scatter | solution.py:275
  865.4 14.6 copy-start.61
  865.4 547.1 %reduce-scatter.17.cloned.1.call-start = ((), (), s32[]{:S(2)}) async-start(), calls=%async_computation.16 | async-start | bytes 13926400 | tf_op jit(solution)/shard_map/reduce_scatter | solution.py:287
  899.8 633.9 %all-reduce.19.cloned.1.call-start = ((), (), s32[]{:S(2)}) async-start(), calls=%async_computation.18 | async-start | bytes 9175040 | tf_op jit(solution)/shard_map/psum | solution.py:309
  1419.8 8.5 copy-start.32
  1419.8 8.5 copy-start.68
  1419.8 8.5 copy-start.73
  1419.8 8.6 copy-start.58
  1419.8 8.6 copy-start.59
  1419.9 8.6 copy-start.56
  1419.9 8.6 copy-start.57
  1419.9 76.4 %copy-start.46 = (bf16[128,1280]{1,0:T(8,128)(2,1)S(1)}, bf16[128,1280]{1,0:T(8,128)(2,1)}, u32[]{:S(2)}) copy-start(bf16[128,1280]{1,0:T(8,128)(2,1)} %copy-done.45) | copy-start | bytes 983044
  1419.9 76.4 %copy-start.48 = (bf16[128,1280]{1,0:T(8,128)(2,1)S(1)}, bf16[128,1280]{1,0:T(8,128)(2,1)}, u32[]{:S(2)}) copy-start(bf16[128,1280]{1,0:T(8,128)(2,1)} %copy-done.47) | copy-start | bytes 983044
  1419.9 77.3 %copy-start.18 = (f32[128,1280]{1,0:T(8,128)S(1)}, f32[128,1280]{1,0:T(8,128)}, u32[]{:S(2)}) copy-start(f32[128,1280]{1,0:T(8,128)} %copy-done.17) | copy-start | bytes 1966084
  1419.9 77.2 %copy-start.20 = (f32[128,1280]{1,0:T(8,128)S(1)}, f32[128,1280]{1,0:T(8,128)}, u32[]{:S(2)}) copy-start(f32[128,1280]{1,0:T(8,128)} %copy-done.19) | copy-start | bytes 1966084
  (49 other events, 146.2 us)
Sparse Core Ops, SparseCore 0:
  10.4 87.1 all-gather.8
  99.9 44.1 all-gather.10
  146.4 102.8 all-gather.12
  251.4 102.1 all-gather.14
  355.7 102.1 all-gather.16
  460.1 102.1 all-gather.18
  662.6 136.5 reduce-scatter.18
  803.4 65.9 reduce-scatter.10
  873.6 113.2 reduce-scatter.8
  990.8 138.1 reduce-scatter.12
  1133.6 137.4 reduce-scatter.14
  1275.1 137.4 reduce-scatter.16
  1416.4 117.3 all-reduce.18
where the time goes:
time: 1560 us; the launch traced here: 1550 us
  waiting for transfers between devices  969 us (62%)
  matrix products  339 us (22%)
  blocking collectives  147 us (9%)
  local copies, waits for them, and re-layouts  41 us (3%)
  other arithmetic  33.2 us (2%)
  between operations  18 us (1%)
    reduce_scatter x1, waiting for transfers between devices, shards(): lax.psum_scatter(totals[3].astype(jnp.bfloat16), 'dp', scatter_dimension=...  142 us
    reduce_scatter x1, waiting for transfers between devices, shards(): lax.psum_scatter(totals[2].astype(jnp.bfloat16), 'dp', scatter_dimension=...  142 us
    reduce_scatter x1, waiting for transfers between devices, shards(): lax.psum_scatter(totals[7].astype(jnp.bfloat16), 'dp', scatter_dimension=...  141 us
    unnamed x3, blocking collectives  133 us
    dot_general x10, matrix products, row_product(): lax.dot_general(left, right, (((0,), (0,)), ((), ())), preferred_element_...  110 us
    all_gather x1, waiting for transfers between devices, shards(): lax.all_gather(up_weight, 'dp', axis=0, tiled=True)  98.3 us
    all_gather x1, waiting for transfers between devices, shards(): lax.all_gather(gene_weight, 'dp', axis=0, tiled=True)  97.8 us
    all_gather x1, waiting for transfers between devices, shards(): lax.all_gather(down_weight, 'dp', axis=0, tiled=True)  96.1 us
  transfers between devices with their start and end apart: 13, of which 11 were waited for; matrix products, arithmetic and copies ran while one was open for 19% of the time, Pallas kernels for 0%

commit v1 on v0

--- a/solution.py
+++ b/solution.py
@@ -8,6 +8,32 @@
 HEAD = 64
 highest = lax.Precision.HIGHEST
 epsilon = 1e-05
+
+
+def match_figure_on(packet, row_dim):
+    arr_next = list(packet.shape[1:])
+    arr_next[row_dim] *= packet.shape[0]
+    return jnp.moveaxis(packet, 0, row_dim).reshape(arr_next)
+
+
+def attach_tables(point, across, along_dim=0):
+    slots = lax.axis_size(across)
+    pieces_in = [(jj, (jj + 1) % slots) for jj in range(slots)]
+    prior, fresh = ([], [])
+    store = [(ix, src_i) for src_i, ix in pieces_in]
+    for u in tuple(range(slots - 1)):
+        if u % 2 == 0:
+            r1 = lax.ppermute(prior[-1] if prior else point, across, pieces_in)
+            prior.append(r1)
+        else:
+            kept_arr = lax.ppermute(fresh[-1] if fresh else point, across, perm=store)
+            fresh.append(kept_arr)
+    newest = jnp.stack([*prior[::-1], point, *fresh])
+    frame_out = len(prior)
+    x_now = lax.axis_index(across)
+    g_now = x_now - frame_out
+    newest = newest[(jnp.arange(slots) - g_now) % slots]
+    return match_figure_on(newest, along_dim)
 
 
 def row_product(left, right):
@@ -226,7 +252,7 @@
             lax.all_gather(attn_gain, "dp", axis=0, tiled=True),
             lax.all_gather(ffn_gain, "dp", axis=0, tiled=True),
             lax.all_gather(up_bias, "dp", axis=0, tiled=True),
-            lax.all_gather(cell_weight, "dp", axis=0, tiled=True),
+            attach_tables(cell_weight, "dp"),
             lax.all_gather(gene_weight, "dp", axis=0, tiled=True),
             lax.all_gather(decoder_bias, "dp", axis=0, tiled=True),
             lax.all_gather(readout, "dp", axis=0, tiled=True),

time: 1560 us -> 1510 us (0.968)
  waiting for transfers between devices: 969 us -> 863 us
  local copies, waits for them, and re-layouts: 41 us -> 73.8 us
  starting transfers between devices: 1.09 us -> 33.3 us
    ppermute x0 -> x15, waiting for transfers between devices: none -> 138 us  [the longest x8 112 us: attach_tables(): r1 = lax.ppermute(prior[-1] if prior else point, across, pieces_in)]
    all_gather x1, waiting for transfers between devices: 98.3 us -> 5.91 us  [shards(): lax.all_gather(up_weight, 'dp', axis=0, tiled=True)]
    all_gather x1 -> x0, waiting for transfers between devices: 82.8 us -> none  [shards(): lax.all_gather(cell_weight, 'dp', axis=0, tiled=True)]
    ppermute x0 -> x15, starting transfers between devices: none -> 32.4 us  [the longest x7 19 us: attach_tables(): kept_arr = lax.ppermute(fresh[-1] if fresh else point, across, perm=store)]
    all_gather x1, waiting for transfers between devices: 31.2 us -> 0.02 us  [shards(): lax.all_gather(out_weight, 'dp', axis=0, tiled=True)]
    all_gather x1, waiting for transfers between devices: 97.8 us -> 72.8 us  [shards(): lax.all_gather(gene_weight, 'dp', axis=0, tiled=True)]
    unnamed x222 -> x247, local copies, waits for them, and re-layouts: 34.9 us -> 54.6 us
    all_gather x1, waiting for transfers between devices: 16.6 us -> 0.01 us  [shards(): lax.all_gather(qkv_weight, 'dp', axis=0, tiled=True)]
  transfers between devices with their start and end apart: 13 -> 27, of which waited for: 11 -> 17; matrix products, arithmetic and copies ran while one was open for 19% -> 22% of each run, Pallas kernels for 0% -> 0%
where the time goes in v1:
time: 1510 us; the launch traced here: 1500 us
  waiting for transfers between devices  863 us (57%)
  matrix products  332 us (22%)
  blocking collectives  149 us (10%)
  local copies, waits for them, and re-layouts  73.8 us (5%)
  starting transfers between devices  33.3 us (2%)
  other arithmetic  33.2 us (2%)
  between operations  18.7 us (1%)
    reduce_scatter x1, waiting for transfers between devices, shards(): lax.psum_scatter(totals[7].astype(jnp.bfloat16), 'dp', scatter_dimension=...  142 us
    reduce_scatter x1, waiting for transfers between devices, shards(): lax.psum_scatter(totals[3].astype(jnp.bfloat16), 'dp', scatter_dimension=...  142 us
    reduce_scatter x1, waiting for transfers between devices, shards(): lax.psum_scatter(totals[2].astype(jnp.bfloat16), 'dp', scatter_dimension=...  142 us
    unnamed x3, blocking collectives  135 us
    dot_general x10, matrix products, row_product(): lax.dot_general(left, right, (((0,), (0,)), ((), ())), preferred_element_...  112 us
    ppermute x8, waiting for transfers between devices, attach_tables(): r1 = lax.ppermute(prior[-1] if prior else point, across, pieces_in)  112 us
    all_gather x1, waiting for transfers between devices, shards(): lax.all_gather(down_weight, 'dp', axis=0, tiled=True)  101 us
    reduce_scatter x1, waiting for transfers between devices, shards(): lax.psum_scatter(totals[0].astype(jnp.bfloat16), 'dp', scatter_dimension=...  82.7 us
  transfers between devices with their start and end apart: 27, of which 17 were waited for; matrix products, arithmetic and copies ran while one was open for 22% of the time, Pallas kernels for 0%

profile of v1, /device:TPU:0, one launch (start us, length us, event | category | flops | bytes accessed | tf_op | source)
XLA Modules:
  0.0 1502.6 jit_solution(4156774575122488580)
XLA Ops:
  10.6 15.4 %collective-permute-done = bf16[80,5120]{1,0:T(8,128)(2,1)S(1)} collective-permute-done((bf16[80,5120]{1,0:T(8,128)(2,1)}, bf16[80,5120]{1,0:T(8,128)(2,1)S(1)}, u32[]{:S(2)}, u32[]{:S(2)}) %collective-permute-start) | collective-permute-done | bytes 819232 | tf_op jit(solution)/shard_map/ppermute | solution.py:26
  26.0 4.4 collective-permute-start.8
  30.4 25.2 %collective-permute-done.1 = bf16[80,5120]{1,0:T(8,128)(2,1)S(1)} collective-permute-done((bf16[80,5120]{1,0:T(8,128)(2,1)S(1)}, bf16[80,5120]{1,0:T(8,128)(2,1)S(1)}, u32[]{:S(2)}, u32[]{:S(2)}) %collective-permute-start.1) | collective-permute-done | bytes 819232 | tf_op jit(solution)/shard_map/ppermute | solution.py:26
  55.7 4.4 collective-permute-start.9
  60.1 26.3 %collective-permute-done.2 = bf16[80,5120]{1,0:T(8,128)(2,1)S(1)} collective-permute-done((bf16[80,5120]{1,0:T(8,128)(2,1)S(1)}, bf16[80,5120]{1,0:T(8,128)(2,1)S(1)}, u32[]{:S(2)}, u32[]{:S(2)}) %collective-permute-start.2) | collective-permute-done | bytes 819232 | tf_op jit(solution)/shard_map/ppermute | solution.py:26
  86.4 4.5 collective-permute-start.10
  90.9 11.2 collective-permute-done.3
  102.1 4.0 collective-permute-start.4
  106.9 13.0 collective-permute-done.4
  120.0 8.4 collective-permute-start.5
  128.9 20.5 %collective-permute-done.5 = bf16[80,5120]{1,0:T(8,128)(2,1)} collective-permute-done((bf16[80,5120]{1,0:T(8,128)(2,1)S(1)}, bf16[80,5120]{1,0:T(8,128)(2,1)}, u32[]{:S(2)}, u32[]{:S(2)}) %collective-permute-start.5) | collective-permute-done | bytes 819232 | tf_op jit(solution)/shard_map/ppermute | solution.py:26
  152.6 66.8 %all-reduce.13 = (bf16[1280]{0:T(1024)(128)(2,1)S(1)}, bf16[5120]{0:T(1024)(128)(2,1)S(1)}, bf16[1280]{0:T(1024)(128)(2,1)S(1)}, bf16[5120]{0:T(1024)(128)(2,1)S(1)}, bf16[5120]{0:T(1024)(128)(2,1)S(1)}) all-reduce(bf16[1280]{0:T(1024)(128)(2,1)S(1)} %dynamic-update-slice.6, ...), channel_id=1, replica_groups=mesh['dp'=16,'query'=2] {'dp'}, use_global_device_ids=true, to_apply=%add | all-reduce | flops 17920 | bytes 71680
  221.3 22.9 %collective-permute-done.13 = bf16[80,5120]{1,0:T(8,128)(2,1)S(1)} collective-permute-done((bf16[80,5120]{1,0:T(8,128)(2,1)}, bf16[80,5120]{1,0:T(8,128)(2,1)S(1)}, u32[]{:S(2)}, u32[]{:S(2)}) %collective-permute-start.13) | collective-permute-done | bytes 819232 | tf_op jit(solution)/shard_map/ppermute | solution.py:29
  244.1 4.6 collective-permute-start.14
  268.4 3.1 collective-permute-done.14
  272.5 11.9 gather_fusion
  284.4 5.3 convolution_convert_fusion.1
  291.0 5.4 convolution_convert_fusion
  308.4 5.9 all-gather.12.cloned.1.call-done
  314.3 8.2 convolution_add_fusion.2
  322.5 101.2 %all-gather.14.cloned.1.call-done = bf16[5120,1280]{1,0:T(8,128)(2,1)} async-done(((bf16[320,1280]{1,0:T(8,128)(2,1)}), bf16[5120,1280]{1,0:T(8,128)(2,1)}) %all-gather.14.cloned.1.call-update) | async-done | bytes 13107216 | tf_op jit(solution)/shard_map/all_gather | solution.py:251
  423.7 8.0 fusion.26
  431.7 4.9 all-gather
  438.7 8.5 fusion.27
  447.2 4.4 all-gather.1
  455.2 72.8 %all-gather.16.cloned.1.call-done = bf16[1280,5120]{1,0:T(8,128)(2,1)} async-done(((bf16[80,5120]{1,0:T(8,128)(2,1)}), bf16[1280,5120]{1,0:T(8,128)(2,1)}) %all-gather.16.cloned.1.call-update) | async-done | bytes 13107216 | tf_op jit(solution)/shard_map/all_gather | solution.py:256
  528.0 8.5 fusion.49
  536.5 3.9 add_add_fusion
  540.5 8.5 fusion.53
  549.0 7.6 multiply_reduce_fusion.3
  557.9 11.2 convert_reduce_fusion.1
  569.1 12.5 fusion.51
  581.6 16.2 %fusion.2 = bf16[1280,5120]{0,1:T(8,128)(2,1)} fusion(f32[5120,1280]{1,0:T(8,128)} %fusion.51, bf16[384,5120]{1,0:T(8,128)(2,1)} %get-tuple-element.137, bf16[2,1,384,1280]{3,2,1,0:T(8,128)(2,1)} %param.34), kind=kOutput, calls=%fused_computation.8 | convolution fusion | flops 5046272000 | bytes 44236800 | tf_op jit(solution)/shard_map/dot_general | solution.py:40
  597.8 17.6 %copy.89 = bf16[1280,5120]{1,0:T(8,128)(2,1)} copy(bf16[1280,5120]{0,1:T(8,128)(2,1)} %fusion.2) | data formatting | bytes 26214400
  618.7 3.1 fusion.135
  623.3 14.1 convolution_convert_fusion.5
  637.5 13.5 convolution_convert_fusion.4
  650.9 8.3 all-reduce.15
  662.1 11.2 convert_reduce_fusion.3
  673.3 10.1 multiply_reduce_fusion.7
  683.4 9.7 convert_reduce_fusion.2
  693.1 10.3 multiply_reduce_fusion.6
  710.3 3.0 convolution_convert_fusion.3
  715.2 3.0 convolution_convert_fusion.2
  724.3 3.2 convolution_bitcast_fusion.4
  729.9 3.2 convolution_bitcast_fusion.2
  733.1 3.1 convolution_bitcast_fusion.1
  738.8 8.3 fusion.116
  747.2 11.2 add_convert_fusion.4
  759.0 13.9 fusion.167
  772.9 18.1 %add_convert_fusion.1 = bf16[1280,5120]{1,0:T(8,128)(2,1)} fusion(f32[1280,5120]{1,0:T(8,128)} %fusion.167, f32[2,5120]{1,0:T(2,128)S(1)} %fusion.134, bf16[2,1,1280]{2,1,0:T(2,128)(2,1)S(1)} %copy-done.75), kind=kOutput, calls=%fused_computation.4 | convolution fusion | flops 170393600 | bytes 39367680 | tf_op jit(solution)/shard_map/dot_general | solution.py:214
  792.1 12.6 fusion.146
  804.7 15.9 %add_convert_fusion.2 = bf16[5120,1280]{1,0:T(8,128)(2,1)} fusion(f32[5120,1280]{1,0:T(8,128)} %fusion.146, f32[128,1280]{1,0:T(8,128)S(1)} %copy-done.22, f32[128,5120]{1,0:T(8,128)} %copy-done.11), kind=kOutput, calls=%fused_computation.5 | convolution fusion | flops 1696890880 | bytes 42598400 | tf_op jit(solution)/shard_map/dot_general | solution.py:40
  821.7 12.8 fusion.187
  834.5 18.8 %add_convert_fusion.3 = bf16[1280,5120]{1,0:T(8,128)(2,1)} fusion(f32[1280,5120]{1,0:T(8,128)} %fusion.187, bf16[128,5120]{1,0:T(8,128)(2,1)} %copy-done.26, f32[128,1280]{1,0:T(8,128)S(1)} %copy-done.6, f32[128]{0:T(128)S(1)} %add_rsqrt_fusion, f32[128]{0:T(128)S(1)} %broadcast_multiply_fusion.8, f32[1280]{0:T(1024)S(1)} %convert_element_type.331), kind=kOutput, calls=%fused_computation.6 | convolution fusion | flops 1691484160 | bytes 41293824 | tf_op jit(solution)/shard_map/dot_general | solution.py:40
  857.0 82.7 %reduce-scatter.9.cloned.1.call-done = bf16[80,3840]{1,0:T(8,128)(2,1)} async-done(((bf16[1280,3840]{1,0:T(8,128)(2,1)}), bf16[80,3840]{1,0:T(8,128)(2,1)}) %reduce-scatter.9.cloned.1.call-update) | async-done | bytes 614416 | tf_op jit(solution)/shard_map/reduce_scatter | solution.py:292
  939.8 142.3 %reduce-scatter.17.cloned.1.call-done = bf16[80,5120]{1,0:T(8,128)(2,1)} async-done(((bf16[1280,5120]{1,0:T(8,128)(2,1)}), bf16[80,5120]{1,0:T(8,128)(2,1)}) %reduce-scatter.17.cloned.1.call-update) | async-done | bytes 819216 | tf_op jit(solution)/shard_map/reduce_scatter | solution.py:313
  1082.1 142.1 %reduce-scatter.15.cloned.1.call-done = bf16[320,1280]{1,0:T(8,128)(2,1)} async-done(((bf16[5120,1280]{1,0:T(8,128)(2,1)}), bf16[320,1280]{1,0:T(8,128)(2,1)}) %reduce-scatter.15.cloned.1.call-update) | async-done | bytes 819216 | tf_op jit(solution)/shard_map/reduce_scatter | solution.py:301
  1224.2 141.6 %reduce-scatter.13.cloned.1.call-done = bf16[80,5120]{1,0:T(8,128)(2,1)} async-done(((bf16[1280,5120]{1,0:T(8,128)(2,1)}), bf16[80,5120]{1,0:T(8,128)(2,1)}) %reduce-scatter.13.cloned.1.call-update) | async-done | bytes 819216 | tf_op jit(solution)/shard_map/reduce_scatter | solution.py:298
  1365.8 7.2 fusion.196
  1373.1 8.3 fusion.81
  1381.6 59.7 %all-reduce.12 = (bf16[1280]{0:T(1024)(128)(2,1)S(1)}, bf16[1280]{0:T(1024)(128)(2,1)S(1)}, bf16[5120]{0:T(1024)(128)(2,1)S(1)}, bf16[5120]{0:T(1024)(128)(2,1)S(1)}, bf16[5120]{0:T(1024)(128)(2,1)S(1)}) all-reduce(bf16[1280]{0:T(1024)(128)(2,1)S(1)} %add_convert_fusion.9, ...), channel_id=8, replica_groups=mesh['dp'=16,'query'=2] {'dp'}, use_global_device_ids=true, to_apply=%region_36.37.clone | all-reduce | flops 17920 | bytes 71680
  1441.7 5.0 all-reduce.14
  1453.1 33.7 %all-reduce.19.cloned.1.call-done = (bf16[80,5120]{0,1:T(8,128)(2,1)}, bf16[80,3840]{1,0:T(8,128)(2,1)}, bf16[80,1280]{1,0:T(8,128)(2,1)}, bf16[80,5120]{1,0:T(8...) async-done(((bf16[80,5120]{0,1:T(8,128)(2,1)}, bf16[80,3840]{1,0:T(8,128)(2,1)}, bf16[80,1280]{1,0:T(8,128)(2,1)}, bf16[80,5120]{1,0:T(8,128)(2,1)}, ...) | async-done | bytes 4096016 | tf_op jit(solution)/shard_map/psum | solution.py:335
  (374 shorter events, 97.1 us)
Async XLA Ops:
  7.2 142.3 %copy-start.93 = (u32[32]{0:T(128)S(1)}, u32[32]{0:T(128)}, u32[]{:S(2)}) copy-start(u32[32]{0:T(128)} %constant.129) | copy-start | bytes 388
  7.2 144.2 %copy-start.95 = (bf16[320]{0:T(512)(128)(2,1)S(1)}, bf16[320]{0:T(512)(128)(2,1)}, u32[]{:S(2)}) copy-start(bf16[320]{0:T(512)(128)(2,1)} %param.33) | copy-start | bytes 1924
  7.2 144.4 %copy-start.96 = (bf16[320]{0:T(512)(128)(2,1)S(1)}, bf16[320]{0:T(512)(128)(2,1)}, u32[]{:S(2)}) copy-start(bf16[320]{0:T(512)(128)(2,1)} %param.29) | copy-start | bytes 1924
  7.2 144.7 %copy-start.97 = (bf16[320]{0:T(512)(128)(2,1)S(1)}, bf16[320]{0:T(512)(128)(2,1)}, u32[]{:S(2)}) copy-start(bf16[320]{0:T(512)(128)(2,1)} %param.32) | copy-start | bytes 1924
  7.2 144.9 %copy-start.98 = (bf16[80]{0:T(256)(128)(2,1)S(1)}, bf16[80]{0:T(256)(128)(2,1)}, u32[]{:S(2)}) copy-start(bf16[80]{0:T(256)(128)(2,1)} %param.27) | copy-start | bytes 484
  7.2 145.1 %copy-start.99 = (bf16[80]{0:T(256)(128)(2,1)S(1)}, bf16[80]{0:T(256)(128)(2,1)}, u32[]{:S(2)}) copy-start(bf16[80]{0:T(256)(128)(2,1)} %param.28) | copy-start | bytes 484
  7.2 212.2 %copy-start.94 = (s32[1,2,1]{1,2,0:T(1,128)S(1)}, s32[1,2,1]{1,2,0:T(1,128)}, u32[]{:S(2)}) copy-start(s32[1,2,1]{1,2,0:T(1,128)} %param.37) | copy-start | bytes 28
  7.3 212.8 %copy-start.91 = (s32[2,1,384]{2,1,0:T(1,128)S(1)}, s32[2,1,384]{2,1,0:T(1,128)}, u32[]{:S(2)}) copy-start(s32[2,1,384]{2,1,0:T(1,128)} %param.35) | copy-start | bytes 9220
  7.3 212.8 %copy-start.92 = (s32[2,1,384]{2,1,0:T(1,128)S(1)}, s32[2,1,384]{2,1,0:T(1,128)}, u32[]{:S(2)}) copy-start(s32[2,1,384]{2,1,0:T(1,128)} %param.36) | copy-start | bytes 9220
  7.3 212.8 %copy-start.7 = (bf16[2,1,128,1280]{3,2,1,0:T(8,128)(2,1)S(1)}, bf16[2,1,128,1280]{3,2,1,0:T(8,128)(2,1)}, u32[]{:S(2)}) copy-start(bf16[2,1,128,1280]{3,2,1,0:T(8,128)(2,1)} %param.21) | copy-start | bytes 1966084
  7.3 277.1 %all-gather.8.cloned.1.call-start = ((), (), s32[]{:S(2)}) async-start(), calls=%async_computation.6 | async-start | bytes 10444800 | tf_op jit(solution)/shard_map/all_gather | solution.py:248
  8.0 293.4 %all-gather.10.cloned.1.call-start = ((), (), s32[]{:S(2)}) async-start(), calls=%async_computation.7 | async-start | bytes 3481600 | tf_op jit(solution)/shard_map/all_gather | solution.py:249
  8.8 305.5 %all-gather.12.cloned.1.call-start = ((), (), s32[]{:S(2)}) async-start(), calls=%async_computation.8 | async-start | bytes 13926400 | tf_op jit(solution)/shard_map/all_gather | solution.py:250
  9.5 414.2 %all-gather.14.cloned.1.call-start = ((), (), s32[]{:S(2)}) async-start(), calls=%async_computation.9 | async-start | bytes 13926400 | tf_op jit(solution)/shard_map/all_gather | solution.py:251
  10.1 517.9 %all-gather.16.cloned.1.call-start = ((), (), s32[]{:S(2)}) async-start(), calls=%async_computation.10 | async-start | bytes 13926400 | tf_op jit(solution)/shard_map/all_gather | solution.py:256
  10.1 15.9 %collective-permute-start = (bf16[80,5120]{1,0:T(8,128)(2,1)}, bf16[80,5120]{1,0:T(8,128)(2,1)S(1)}, u32[]{:S(2)}, u32[]{:S(2)}) collective-permute-start(bf16[80,5120]{1,0:T(8,128)(2,1)} %param.30), channel_id=1, source_target_pairs={{0,2},{2,4},{4,6},{6,8},{8,10},{10,12},{12,14},{14,16},{16,18},{18... | collective-permute-start | bytes 2457608 | tf_op jit(solution)/shard_map/ppermute | solution.py:26
  26.0 29.6 %collective-permute-start.1 = (bf16[80,5120]{1,0:T(8,128)(2,1)S(1)}, bf16[80,5120]{1,0:T(8,128)(2,1)S(1)}, u32[]{:S(2)}, u32[]{:S(2)}) collective-permute-start(bf16[80,5120]{1,0:T(8,128)(2,1)S(1)} %collective-permute-done), channel_id=1, source_target_pairs={{0,2},{2,4},{4,6},{6,8},{8,10},{10,12},{12,14},{14,16},{16,18},{18... | collective-permute-start | bytes 2457608 | tf_op jit(solution)/shard_map/ppermute | solution.py:26
  26.0 29.6 %collective-permute-start.8 = (bf16[80,5120]{1,0:T(8,128)(2,1)}, bf16[80,5120]{1,0:T(8,128)(2,1)S(1)}, u32[]{:S(2)}, u32[]{:S(2)}) collective-permute-start(bf16[80,5120]{1,0:T(8,128)(2,1)} %param.30), channel_id=1, source_target_pairs={{2,0},{4,2},{6,4},{8,6},{10,8},{12,10},{14,12},{16,14},{18,16},{20... | collective-permute-start | bytes 2457608 | tf_op jit(solution)/shard_map/ppermute | solution.py:29
  55.6 30.8 %copy-start.42 = (bf16[80,5120]{1,0:T(8,128)(2,1)}, bf16[80,5120]{1,0:T(8,128)(2,1)S(1)}, u32[]{:S(2)}) copy-start(bf16[80,5120]{1,0:T(8,128)(2,1)S(1)} %collective-permute-done.1) | copy-start | bytes 2457604
  55.6 30.8 %collective-permute-start.2 = (bf16[80,5120]{1,0:T(8,128)(2,1)S(1)}, bf16[80,5120]{1,0:T(8,128)(2,1)S(1)}, u32[]{:S(2)}, u32[]{:S(2)}) collective-permute-start(bf16[80,5120]{1,0:T(8,128)(2,1)S(1)} %collective-permute-done.1), channel_id=1, source_target_pairs={{0,2},{2,4},{4,6},{6,8},{8,10},{10,12},{12,14},{14,16},{16,18},{18... | collective-permute-start | bytes 2457608 | tf_op jit(solution)/shard_map/ppermute | solution.py:26
  55.6 196.5 %copy-start.40 = (bf16[80,5120]{1,0:T(8,128)(2,1)}, bf16[80,5120]{1,0:T(8,128)(2,1)S(1)}, u32[]{:S(2)}) copy-start(bf16[80,5120]{1,0:T(8,128)(2,1)S(1)} %collective-permute-done.8) | copy-start | bytes 2457604
  55.7 30.8 %collective-permute-start.9 = (bf16[80,5120]{1,0:T(8,128)(2,1)S(1)}, bf16[80,5120]{1,0:T(8,128)(2,1)S(1)}, u32[]{:S(2)}, u32[]{:S(2)}) collective-permute-start(bf16[80,5120]{1,0:T(8,128)(2,1)S(1)} %collective-permute-done.8), channel_id=1, source_target_pairs={{2,0},{4,2},{6,4},{8,6},{10,8},{12,10},{14,12},{16,14},{18,16},{20... | collective-permute-start | bytes 2457608 | tf_op jit(solution)/shard_map/ppermute | solution.py:29
  86.4 19.6 %copy-start.46 = (bf16[80,5120]{1,0:T(8,128)(2,1)}, bf16[80,5120]{1,0:T(8,128)(2,1)S(1)}, u32[]{:S(2)}) copy-start(bf16[80,5120]{1,0:T(8,128)(2,1)S(1)} %collective-permute-done.2) | copy-start | bytes 2457604
  86.4 15.7 %collective-permute-start.3 = (bf16[80,5120]{1,0:T(8,128)(2,1)S(1)}, bf16[80,5120]{1,0:T(8,128)(2,1)S(1)}, u32[]{:S(2)}, u32[]{:S(2)}) collective-permute-start(bf16[80,5120]{1,0:T(8,128)(2,1)S(1)} %collective-permute-done.2), channel_id=1, source_target_pairs={{0,2},{2,4},{4,6},{6,8},{8,10},{10,12},{12,14},{14,16},{16,18},{18... | collective-permute-start | bytes 2457608 | tf_op jit(solution)/shard_map/ppermute | solution.py:26
  86.4 19.6 %collective-permute-start.10 = (bf16[80,5120]{1,0:T(8,128)(2,1)S(1)}, bf16[80,5120]{1,0:T(8,128)(2,1)S(1)}, u32[]{:S(2)}, u32[]{:S(2)}) collective-permute-start(bf16[80,5120]{1,0:T(8,128)(2,1)S(1)} %collective-permute-done.9), channel_id=1, source_target_pairs={{2,0},{4,2},{6,4},{8,6},{10,8},{12,10},{14,12},{16,14},{18,16},{20... | collective-permute-start | bytes 2457608 | tf_op jit(solution)/shard_map/ppermute | solution.py:29
  102.1 26.3 %copy-start.50 = (bf16[80,5120]{1,0:T(8,128)(2,1)}, bf16[80,5120]{1,0:T(8,128)(2,1)S(1)}, u32[]{:S(2)}) copy-start(bf16[80,5120]{1,0:T(8,128)(2,1)S(1)} %collective-permute-done.3) | copy-start | bytes 2457604
  102.1 17.9 %collective-permute-start.4 = (bf16[80,5120]{1,0:T(8,128)(2,1)S(1)}, bf16[80,5120]{1,0:T(8,128)(2,1)S(1)}, u32[]{:S(2)}, u32[]{:S(2)}) collective-permute-start(bf16[80,5120]{1,0:T(8,128)(2,1)S(1)} %collective-permute-done.3), channel_id=1, source_target_pairs={{0,2},{2,4},{4,6},{6,8},{8,10},{10,12},{12,14},{14,16},{16,18},{18... | collective-permute-start | bytes 2457608 | tf_op jit(solution)/shard_map/ppermute | solution.py:26
  106.0 22.3 %collective-permute-start.11 = (bf16[80,5120]{1,0:T(8,128)(2,1)S(1)}, bf16[80,5120]{1,0:T(8,128)(2,1)}, u32[]{:S(2)}, u32[]{:S(2)}) collective-permute-start(bf16[80,5120]{1,0:T(8,128)(2,1)S(1)} %collective-permute-done.10), channel_id=1, source_target_pairs={{2,0},{4,2},{6,4},{8,6},{10,8},{12,10},{14,12},{16,14},{18,16},{20... | collective-permute-start | bytes 2457608 | tf_op jit(solution)/shard_map/ppermute | solution.py:29
  120.0 29.4 %collective-permute-start.5 = (bf16[80,5120]{1,0:T(8,128)(2,1)S(1)}, bf16[80,5120]{1,0:T(8,128)(2,1)}, u32[]{:S(2)}, u32[]{:S(2)}) collective-permute-start(bf16[80,5120]{1,0:T(8,128)(2,1)S(1)} %collective-permute-done.4), channel_id=1, source_target_pairs={{0,2},{2,4},{4,6},{6,8},{8,10},{10,12},{12,14},{14,16},{16,18},{18... | collective-permute-start | bytes 2457608 | tf_op jit(solution)/shard_map/ppermute | solution.py:26
  128.4 91.9 %collective-permute-start.12 = (bf16[80,5120]{1,0:T(8,128)(2,1)}, bf16[80,5120]{1,0:T(8,128)(2,1)}, u32[]{:S(2)}, u32[]{:S(2)}) collective-permute-start(bf16[80,5120]{1,0:T(8,128)(2,1)} %collective-permute-done.11), channel_id=1, source_target_pairs={{2,0},{4,2},{6,4},{8,6},{10,8},{12,10},{14,12},{16,14},{18,16},{20... | collective-permute-start | bytes 2457608 | tf_op jit(solution)/shard_map/ppermute | solution.py:29
  149.3 71.0 %collective-permute-start.6 = (bf16[80,5120]{1,0:T(8,128)(2,1)}, bf16[80,5120]{1,0:T(8,128)(2,1)}, u32[]{:S(2)}, u32[]{:S(2)}) collective-permute-start(bf16[80,5120]{1,0:T(8,128)(2,1)} %collective-permute-done.5), channel_id=1, source_target_pairs={{0,2},{2,4},{4,6},{6,8},{8,10},{10,12},{12,14},{14,16},{16,18},{18... | collective-permute-start | bytes 2457608 | tf_op jit(solution)/shard_map/ppermute | solution.py:26
  149.4 705.3 %reduce-scatter.19.cloned.1.call-start = ((), (), s32[]{:S(2)}) async-start(), calls=%async_computation.16 | async-start | bytes 13926400
  219.4 71.6 %copy-start.57 = (f32[1280]{0:T(1024)}, f32[1280]{0:T(1024)S(1)}, u32[]{:S(2)}) copy-start(f32[1280]{0:T(1024)S(1)} %convert_element_type.325) | copy-start | bytes 15364
  220.3 23.8 %collective-permute-start.13 = (bf16[80,5120]{1,0:T(8,128)(2,1)}, bf16[80,5120]{1,0:T(8,128)(2,1)S(1)}, u32[]{:S(2)}, u32[]{:S(2)}) collective-permute-start(bf16[80,5120]{1,0:T(8,128)(2,1)} %collective-permute-done.12), channel_id=1, source_target_pairs={{2,0},{4,2},{6,4},{8,6},{10,8},{12,10},{14,12},{16,14},{18,16},{20... | collective-permute-start | bytes 2457608 | tf_op jit(solution)/shard_map/ppermute | solution.py:29
  220.4 28.6 %collective-permute-start.7 = (bf16[80,5120]{1,0:T(8,128)(2,1)}, bf16[80,5120]{1,0:T(8,128)(2,1)S(1)}, u32[]{:S(2)}, u32[]{:S(2)}) collective-permute-start(bf16[80,5120]{1,0:T(8,128)(2,1)} %collective-permute-done.6), channel_id=1, source_target_pairs={{0,2},{2,4},{4,6},{6,8},{8,10},{10,12},{12,14},{14,16},{16,18},{18... | collective-permute-start | bytes 2457608 | tf_op jit(solution)/shard_map/ppermute | solution.py:26
  220.9 63.5 %copy-start.82 = (f32[128]{0:T(128)}, f32[128]{0:T(128)S(1)}, u32[]{:S(2)}) copy-start(f32[128]{0:T(128)S(1)} %get-tuple-element.160) | copy-start | bytes 1540
  220.9 70.2 %copy-start.85 = (f32[128]{0:T(128)}, f32[128]{0:T(128)S(1)}, u32[]{:S(2)}) copy-start(f32[128]{0:T(128)S(1)} %get-tuple-element.159) | copy-start | bytes 1540
  221.2 33.4 %copy-start.53 = (bf16[80,5120]{1,0:T(8,128)(2,1)S(1)}, bf16[80,5120]{1,0:T(8,128)(2,1)}, u32[]{:S(2)}) copy-start(bf16[80,5120]{1,0:T(8,128)(2,1)} %copy-done.52) | copy-start | bytes 2457604
  221.2 63.2 %copy-start.87 = (f32[128]{0:T(128)}, f32[128]{0:T(128)S(1)}, u32[]{:S(2)}) copy-start(f32[128]{0:T(128)S(1)} %add_rsqrt_fusion.3) | copy-start | bytes 1540
  221.2 69.8 %copy-start.89 = (f32[128]{0:T(128)}, f32[128]{0:T(128)S(1)}, u32[]{:S(2)}) copy-start(f32[128]{0:T(128)S(1)} %add_rsqrt_fusion.1) | copy-start | bytes 1540
  244.1 27.5 %collective-permute-start.14 = (bf16[80,5120]{1,0:T(8,128)(2,1)S(1)}, bf16[80,5120]{1,0:T(8,128)(2,1)S(1)}, u32[]{:S(2)}, u32[]{:S(2)}) collective-permute-start(bf16[80,5120]{1,0:T(8,128)(2,1)S(1)} %collective-permute-done.13), channel_id=1, source_target_pairs={{2,0},{4,2},{6,4},{8,6},{10,8},{12,10},{14,12},{16,14},{18,16},{20... | collective-permute-start | bytes 2457608 | tf_op jit(solution)/shard_map/ppermute | solution.py:29
  304.2 388.9 %copy-start.9 = (f32[128,1280]{1,0:T(8,128)}, f32[128,1280]{1,0:T(8,128)S(1)}, u32[]{:S(2)}) copy-start(f32[128,1280]{1,0:T(8,128)S(1)} %get-tuple-element.150) | copy-start | bytes 1966084
  308.1 396.4 %copy-start.5 = (f32[128,1280]{1,0:T(8,128)}, f32[128,1280]{1,0:T(8,128)S(1)}, u32[]{:S(2)}) copy-start(f32[128,1280]{1,0:T(8,128)S(1)} %get-tuple-element.146) | copy-start | bytes 1966084
  423.7 12.9 copy-start
  436.6 15.0 copy-start.76
  436.6 15.0 slice-start
  436.6 15.0 slice-start.1
  438.6 13.0 slice-start.2
  438.6 13.0 slice-start.3
  615.4 241.7 %reduce-scatter.11.cloned.1.call-start = ((), (), s32[]{:S(2)}) async-start(), calls=%async_computation.12 | async-start | bytes 3481600 | tf_op jit(solution)/shard_map/reduce_scatter | solution.py:295
  660.9 43.7 %copy-start.21 = (f32[128,1280]{1,0:T(8,128)}, f32[128,1280]{1,0:T(8,128)S(1)}, u32[]{:S(2)}) copy-start(f32[128,1280]{1,0:T(8,128)S(1)} %scatter-add.9) | copy-start | bytes 1966084
  662.1 31.0 %copy-start.23 = (f32[128,1280]{1,0:T(8,128)}, f32[128,1280]{1,0:T(8,128)S(1)}, u32[]{:S(2)}) copy-start(f32[128,1280]{1,0:T(8,128)S(1)} %scatter-add.6) | copy-start | bytes 1966084
  708.4 231.4 %reduce-scatter.9.cloned.1.call-start = ((), (), s32[]{:S(2)}) async-start(), calls=%async_computation.11 | async-start | bytes 10444800 | tf_op jit(solution)/shard_map/reduce_scatter | solution.py:292
  758.4 14.5 copy-start.75
  758.4 323.7 %reduce-scatter.17.cloned.1.call-start = ((), (), s32[]{:S(2)}) async-start(), calls=%async_computation.15 | async-start | bytes 13926400 | tf_op jit(solution)/shard_map/reduce_scatter | solution.py:313
  791.0 13.7 copy-start.22
  791.0 433.1 %reduce-scatter.15.cloned.1.call-start = ((), (), s32[]{:S(2)}) async-start(), calls=%async_computation.14 | async-start | bytes 13926400 | tf_op jit(solution)/shard_map/reduce_scatter | solution.py:301
  820.6 13.9 copy-start.6
  820.6 545.2 %reduce-scatter.13.cloned.1.call-start = ((), (), s32[]{:S(2)}) async-start(), calls=%async_computation.13 | async-start | bytes 13926400 | tf_op jit(solution)/shard_map/reduce_scatter | solution.py:298
  853.3 633.5 %all-reduce.19.cloned.1.call-start = ((), (), s32[]{:S(2)}) async-start(), calls=%async_computation.17 | async-start | bytes 9175040 | tf_op jit(solution)/shard_map/psum | solution.py:335
  1373.1 76.3 %copy-start.60 = (bf16[128,1280]{1,0:T(8,128)(2,1)S(1)}, bf16[128,1280]{1,0:T(8,128)(2,1)}, u32[]{:S(2)}) copy-start(bf16[128,1280]{1,0:T(8,128)(2,1)} %copy-done.59) | copy-start | bytes 983044
  1373.1 76.3 %copy-start.62 = (bf16[128,1280]{1,0:T(8,128)(2,1)S(1)}, bf16[128,1280]{1,0:T(8,128)(2,1)}, u32[]{:S(2)}) copy-start(bf16[128,1280]{1,0:T(8,128)(2,1)} %copy-done.61) | copy-start | bytes 983044
  1373.1 77.2 %copy-start.18 = (f32[128,1280]{1,0:T(8,128)S(1)}, f32[128,1280]{1,0:T(8,128)}, u32[]{:S(2)}) copy-start(f32[128,1280]{1,0:T(8,128)} %copy-done.17) | copy-start | bytes 1966084
  1373.1 77.2 %copy-start.20 = (f32[128,1280]{1,0:T(8,128)S(1)}, f32[128,1280]{1,0:T(8,128)}, u32[]{:S(2)}) copy-start(f32[128,1280]{1,0:T(8,128)} %copy-done.19) | copy-start | bytes 1966084
  (68 other events, 290.6 us)
Sparse Core Ops, SparseCore 0:
  10.4 132.1 all-gather.7
  144.9 53.4 all-gather.9
  200.7 113.5 all-gather.11
  316.4 107.2 all-gather.13
  425.8 102.1 all-gather.15
  615.5 136.5 reduce-scatter.18
  756.4 65.9 reduce-scatter.10
  826.5 113.2 reduce-scatter.8
  943.9 138.1 reduce-scatter.16
  1086.6 137.5 reduce-scatter.14
  1228.3 137.4 reduce-scatter.12
  1369.5 117.2 all-reduce.18
